TPU v7x, 128 devices: a whole 4x4x4 slice. The times are simulated.
128 devices in a mesh: row: 4 (over z), col: 16 (over y, x_lo, core), depth: 2 (over x_hi).
Axes of the slice: x: 4 (x_hi: 2, x_lo: 2; x = x_hi * 2 + x_lo), y: 4, z: 4, core: 2. Of those that a mesh axis runs over, the one named last changes fastest.
Arguments:
- layer_input: bfloat16 [1536, 6144], P(('depth', 'col'), 'row'), may hold values from -6 to 6
- w_in: bfloat16 [6144, 24576], P('row', 'col'), may hold values from -0.078125 to 0.078125
- w_out: bfloat16 [24576, 6144], P('col', 'row'), may hold values from -0.0390625 to 0.0390625
- out_grad: bfloat16 [1536, 6144], P(('depth', 'col'), 'row'), may hold values from -0.95703125 to 0.95703125
- drop_seed: int32 [1], replicated, may hold values from 0 to 1073741823
- drop_step: int32 [1], replicated, may hold values from 0 to 999999
Outputs:
- input_grad: float32 [1536, 6144], P(('depth', 'col'), 'row')
- w_in_grad: float32 [6144, 24576], P('row', ('col', 'depth'))
- w_out_grad: float32 [24576, 6144], P('col', ('row', 'depth'))
All inputs are finite; a program needn't handle non-finite values.
Results may differ from a plain program's by a relative error of at most 0.0041.
Values may be sent and summed in bfloat16 or wider, within the bound.
A program may use at most 128 MiB of HBM per device.

v0:
```python
import math

import jax
import jax.numpy as jnp
from jax import lax
from jax.sharding import PartitionSpec as P

D = 6144


keep_scale = 1.0 / 0.9
gelu_coef = math.sqrt(2.0 / math.pi)


def mix_bits(word_bits):
    word_bits = word_bits ^ lax.shift_right_logical(word_bits, jnp.int32(16))
    word_bits = word_bits * jnp.int32(2146121005)
    word_bits = word_bits ^ lax.shift_right_logical(word_bits, jnp.int32(15))
    word_bits = word_bits * jnp.int32(-2073254261)
    word_bits = word_bits ^ lax.shift_right_logical(word_bits, jnp.int32(16))
    return word_bits


def keep_mask(drop_seed, drop_step, row_start, col_start, row_count, col_count, row_length):
    stream_key = mix_bits(mix_bits(drop_step[0] + jnp.int32(1013904223)) ^ drop_seed[0])
    row_ids = jnp.arange(row_count, dtype=jnp.int32) + row_start
    col_ids = jnp.arange(col_count, dtype=jnp.int32) + col_start
    flat_index = row_ids[:, None] * jnp.int32(row_length) + col_ids[None, :]
    hashed = mix_bits(flat_index ^ stream_key)
    return hashed & jnp.int32(16777215) < jnp.int32(15099494)


def gelu_parts(hidden_pre):
    inner_arg = gelu_coef * (hidden_pre + 0.044715 * hidden_pre * hidden_pre * hidden_pre)
    tanh_val = jnp.tanh(inner_arg)
    act_full = 0.5 * hidden_pre * (1.0 + tanh_val)
    gelu_slope = 0.5 * (1.0 + tanh_val) + 0.5 * hidden_pre * (
        1.0 - tanh_val * tanh_val
    ) * gelu_coef * (1.0 + 3.0 * 0.044715 * hidden_pre * hidden_pre)
    return (act_full, gelu_slope)


def contract_rows(left, right):
    return lax.dot_general(
        left, right, (((0,), (0,)), ((), ())), preferred_element_type=jnp.float32
    )


def contract_cols(left, right):
    return lax.dot_general(
        left, right, (((1,), (1,)), ((), ())), preferred_element_type=jnp.float32
    )


def per_device(layer_input, w_in, w_out, out_grad, drop_seed, drop_step):
    whole_in, whole_grad = (
        lax.all_gather(layer_input, "col", axis=0, tiled=True),
        lax.all_gather(out_grad, "col", axis=0, tiled=True),
    )
    token_group = whole_in.shape[0]
    feature_span = whole_in.shape[1]
    row_start = lax.axis_index("depth") * token_group
    col_start = lax.axis_index("row") * feature_span
    keep_flags = keep_mask(drop_seed, drop_step, row_start, col_start, token_group, feature_span, D)
    scaled = jnp.where(
        keep_flags, whole_grad.astype(jnp.float32) * keep_scale, jnp.zeros((), jnp.float32)
    ).astype(jnp.bfloat16)
    partial_pre = jnp.dot(whole_in, w_in, preferred_element_type=jnp.float32)
    partial_act = contract_cols(scaled, w_out)
    hidden_pre, act_grad = lax.psum((partial_pre, partial_act), "row")
    act_full, gelu_slope = gelu_parts(hidden_pre)
    hidden_act = act_full.astype(jnp.bfloat16)
    pre_grad = (act_grad * gelu_slope).astype(jnp.bfloat16)
    out_term = contract_rows(hidden_act, scaled)
    in_term = contract_rows(whole_in, pre_grad)
    out_total, in_total = (
        lax.psum_scatter(out_term, "depth", scatter_dimension=1, tiled=True),
        lax.psum_scatter(in_term, "depth", scatter_dimension=1, tiled=True),
    )
    input_grad = lax.psum_scatter(
        contract_cols(pre_grad, w_in), "col", scatter_dimension=0, tiled=True
    )
    return (input_grad, in_total, out_total)


def solution(mesh):
    placed = (
        P(("depth", "col"), "row"),
        P("row", "col"),
        P("col", "row"),
        P(("depth", "col"), "row"),
        P(),
        P(),
    )
    return jax.shard_map(
        per_device,
        mesh=mesh,
        in_specs=placed,
        out_specs=(
            P(("depth", "col"), "row"),
            P("row", ("col", "depth")),
            P("col", ("row", "depth")),
        ),
        check_vma=False,
    )
```

profile of v0, /device:TPU:1, one launch (start us, length us, event | category | flops | bytes accessed | tf_op | source)
XLA Modules:
  0.0 595.2 jit_solution(16327440699595015350)
XLA Ops:
  7.2 0.0 all-gather.5.cloned.1.call-start
  7.2 0.7 all-gather.5.cloned.1.call-update
  7.9 0.0 all-gather.3.cloned.1.call-start
  7.9 0.7 all-gather.3.cloned.1.call-update
  8.6 0.0 all-reduce.3.cloned.1.call-start
  10.0 37.4 %all-gather.5.cloned.1.call-done = bf16[768,1536]{1,0:T(8,128)(2,1)} async-done(((bf16[48,1536]{1,0:T(8,128)(2,1)}), bf16[768,1536]{1,0:T(8,128)(2,1)}) %all-gather.5.cloned.1.call-update) | async-done | bytes 2359312 | tf_op jit(solution)/shard_map/all_gather | solution.py:57
  47.5 9.1 %fusion.21 = f32[768,1536]{1,0:T(8,128)} fusion(bf16[768,1536]{1,0:T(8,128)(2,1)} %all-gather.5.cloned.1.call-done, bf16[1536,1536]{1,0:T(8,128)(2,1)} %param.7), kind=kOutput, calls=%fused_computation.31 | convolution fusion | flops 3623878656 | bytes 11796480 | tf_op jit(solution)/shard_map/dot_general | solution.py:68
  56.5 26.9 %all-gather.3.cloned.1.call-done = bf16[768,1536]{1,0:T(8,128)(2,1)} async-done(((bf16[48,1536]{1,0:T(8,128)(2,1)}), bf16[768,1536]{1,0:T(8,128)(2,1)}) %all-gather.3.cloned.1.call-update) | async-done | bytes 2359312 | tf_op jit(solution)/shard_map/all_gather | solution.py:58
  83.4 10.2 %fusion.20 = f32[768,1536]{1,0:T(8,128)} fusion(bf16[1536,1536]{1,0:T(8,128)(2,1)} %param.8, bf16[768,1536]{1,0:T(8,128)(2,1)} %all-gather.3.cloned.1.call-done, s32[]{:T(128)S(6)} %xor.42, s32[1536]{0:T(1024)S(1)} %iota_add_fusion, s32[768]{0:T(1024)S(1)} %add_multiply_fusion), kind=kOutput, calls=%fused_computation.30 | convolution fusion | flops 3642753024 | bytes 11805700 | tf_op jit(solution)/shard_map/dot_general | solution.py:50
  93.6 0.0 reduce-scatter.6.cloned.1.call-start
  93.7 177.0 %all-reduce.3.cloned.1.call-done = (f32[768,1536]{1,0:T(8,128)}, f32[768,1536]{1,0:T(8,128)}) async-done(((f32[768,1536]{1,0:T(8,128)}, f32[768,1536]{1,0:T(8,128)}), (f32[768,1536]{1,0:T(8,128)}, f32[768,1536]{1,0:T(8,128)})) %all-reduce.3.cloned.1.call-update) | async-done | bytes 9437200 | tf_op jit(solution)/shard_map/psum | solution.py:70
  270.6 5.5 fusion.10
  276.2 6.7 %convolution_bitcast_fusion = f32[1536,1536]{0,1:T(8,128)} fusion(bf16[768,1536]{1,0:T(8,128)(2,1)S(1)} %fusion.10, bf16[768,1536]{1,0:T(8,128)(2,1)S(1)} %copy-done.1), kind=kOutput, calls=%fused_computation | convolution fusion | flops 3623878656 | bytes 14155776 | tf_op jit(solution)/shard_map/dot_general | solution.py:44
  282.9 0.0 reduce-scatter.4.cloned.1.call-start
  282.9 7.8 %fusion.22 = f32[768,1536]{1,0:T(8,128)} fusion(bf16[768,1536]{1,0:T(8,128)(2,1)S(1)} %fusion.10, bf16[1536,1536]{1,0:T(8,128)(2,1)} %param.7), kind=kOutput, calls=%fused_computation.32 | convolution fusion | flops 3623878656 | bytes 11796480 | tf_op jit(solution)/shard_map/dot_general | solution.py:50
  290.8 0.0 reduce-scatter.4.cloned.1.call-update
  290.8 0.2 reduce-scatter.8.cloned.1.call-start
  291.0 2.0 copy-done
  293.0 12.4 %fusion.11 = f32[1536,1536]{1,0:T(8,128)} fusion(f32[768,1536]{1,0:T(8,128)} %get-tuple-element.7, bf16[768,1536]{1,0:T(8,128)(2,1)S(1)} %copy-done, s32[]{:T(128)S(6)} %xor.42, s32[1536]{0:T(1024)S(1)} %iota_add_fusion, s32[768]{0:T(1024)S(1)} %add_multiply_fusion), kind=kOutput, calls=%fused_computation.19 | convolution fusion | flops 3653369856 | bytes 16524292 | tf_op jit(solution)/shard_map/dot_general | solution.py:44
  305.4 0.0 reduce-scatter.8.cloned.1.call-update
  305.5 91.9 %reduce-scatter.6.cloned.1.call-done = f32[1536,768]{0,1:T(8,128)} async-done(((f32[1536,1536]{0,1:T(8,128)}), f32[1536,768]{0,1:T(8,128)}) %reduce-scatter.6.cloned.1.call-update) | async-done | bytes 4718608 | tf_op jit(solution)/shard_map/reduce_scatter | solution.py:78
  397.4 6.0 %copy.9 = f32[1536,768]{1,0:T(8,128)} copy(f32[1536,768]{0,1:T(8,128)} %reduce-scatter.6.cloned.1.call-done) | data formatting | bytes 9437184
  403.4 66.2 %reduce-scatter.4.cloned.1.call-done = f32[48,1536]{1,0:T(8,128)} async-done(((f32[768,1536]{1,0:T(8,128)}), f32[48,1536]{1,0:T(8,128)}) %reduce-scatter.4.cloned.1.call-update) | async-done | bytes 294928 | tf_op jit(solution)/shard_map/reduce_scatter | solution.py:80
  469.6 118.8 %reduce-scatter.8.cloned.1.call-done = f32[1536,768]{1,0:T(8,128)} async-done(((f32[1536,1536]{1,0:T(8,128)}), f32[1536,768]{1,0:T(8,128)}) %reduce-scatter.8.cloned.1.call-update) | async-done | bytes 4718608 | tf_op jit(solution)/shard_map/reduce_scatter | solution.py:77
  (7 shorter events, 0.0 us)
Async XLA Ops:
  7.2 40.3 %all-gather.5.cloned.1.call-start = ((), (), s32[]{:S(2)}) async-start(), calls=%async_computation.4 | async-start | bytes 2506752 | tf_op jit(solution)/shard_map/all_gather | solution.py:57
  7.9 75.5 %all-gather.3.cloned.1.call-start = ((), (), s32[]{:S(2)}) async-start(), calls=%async_computation.3 | async-start | bytes 2506752 | tf_op jit(solution)/shard_map/all_gather | solution.py:58
  8.6 262.0 %all-reduce.3.cloned.1.call-start = ((), (), s32[]{:S(2)}) async-start(), calls=%async_computation.8 | async-start | bytes 18874368 | tf_op jit(solution)/shard_map/psum | solution.py:70
  93.6 303.8 %reduce-scatter.6.cloned.1.call-start = ((), (), s32[]{:S(2)}) async-start(), calls=%async_computation.6 | async-start | bytes 14155776 | tf_op jit(solution)/shard_map/reduce_scatter | solution.py:78
  270.6 5.5 copy-start.1
  282.9 186.7 %reduce-scatter.4.cloned.1.call-start = ((), (), s32[]{:S(2)}) async-start(), calls=%async_computation.5 | async-start | bytes 5013504 | tf_op jit(solution)/shard_map/reduce_scatter | solution.py:80
  290.8 2.3 copy-start
  290.8 297.6 %reduce-scatter.8.cloned.1.call-start = ((), (), s32[]{:S(2)}) async-start(), calls=%async_computation.7 | async-start | bytes 14155776 | tf_op jit(solution)/shard_map/reduce_scatter | solution.py:77
Sparse Core Ops, SparseCore 0:
  9.7 37.7 all-gather.4
  49.2 34.1 all-gather.2
  93.7 176.8 all-reduce.2
  283.0 114.3 reduce-scatter.5
  400.2 69.3 reduce-scatter.3
  472.4 115.9 reduce-scatter.7
where the time goes:
time: 596 us; the launch traced here: 595 us
  waiting for transfers between devices  520 us (87%)
  matrix products  46.2 us (8%)
  between operations  15.4 us (3%)
  local copies, waits for them, and re-layouts  8.04 us (1%)
    psum x1, waiting for transfers between devices, per_device(): hidden_pre, act_grad = lax.psum((partial_pre, partial_act), 'row')  177 us
    reduce_scatter x1, waiting for transfers between devices, per_device(): lax.psum_scatter(out_term, 'depth', scatter_dimension=1, tiled=True)  119 us
    reduce_scatter x1, waiting for transfers between devices, per_device(): lax.psum_scatter(in_term, 'depth', scatter_dimension=1, tiled=True)  91.9 us
    reduce_scatter x1, waiting for transfers between devices, per_device(): lax.psum_scatter(contract_cols(pre_grad, w_in), 'col', scatter_dimension=...  66.2 us
    all_gather x1, waiting for transfers between devices, per_device(): lax.all_gather(layer_input, 'col', axis=0, tiled=True)  37.4 us
    all_gather x1, waiting for transfers between devices, per_device(): lax.all_gather(out_grad, 'col', axis=0, tiled=True)  26.9 us
    dot_general x2, matrix products, contract_rows(): lax.dot_general(left, right, (((0,), (0,)), ((), ())), preferred_element_...  19.1 us
    dot_general x2, matrix products, contract_cols(): lax.dot_general(left, right, (((1,), (1,)), ((), ())), preferred_element_...  18.1 us
  transfers between devices with their start and end apart: 6, of which 6 were waited for; matrix products, arithmetic and copies ran while one was open for 6% of the time, Pallas kernels for 0%

commit v1 on v0

v1 whole, which is shorter than its diff:
```python
import math

import jax
import jax.numpy as jnp
from jax import lax
from jax.experimental import pallas as pl
from jax.experimental.pallas import tpu as pltpu
from jax.sharding import PartitionSpec as P

D = 6144
keep_scale = 1.0 / 0.9
gelu_coef = math.sqrt(2.0 / math.pi)
F32, BF16, I32 = jnp.float32, jnp.bfloat16, jnp.int32
MESH = pl.DeviceIdType.MESH

OWN = 48
CH = 384
QT = 96
HID = 768
FEAT = 1536
ITEMS = [(0, 0), (0, 1), (0, 3), (0, 2), (1, 2), (1, 1), (1, 3), (1, 0)]
N_SEMS = 400

NN = (((1,), (0,)), ((), ()))
NT = (((1,), (1,)), ((), ()))


def mix_bits(v):
    v = v ^ lax.shift_right_logical(v, jnp.int32(16))
    v = v * jnp.int32(2146121005)
    v = v ^ lax.shift_right_logical(v, jnp.int32(15))
    v = v * jnp.int32(-2073254261)
    v = v ^ lax.shift_right_logical(v, jnp.int32(16))
    return v


def gelu_parts(h):
    inner_arg = gelu_coef * (h + 0.044715 * h * h * h)
    t = jnp.tanh(inner_arg)
    act = 0.5 * h * (1.0 + t)
    slope = 0.5 * (1.0 + t) + 0.5 * h * (1.0 - t * t) * gelu_coef * (1.0 + 3.0 * 0.044715 * h * h)
    return act, slope


def slot(b, region, a):
    return pl.ds(((b * 2 + region) * 4 + a) * OWN, OWN)


def kernel(
    x_hbm, win_hbm, wout_hbm, og_hbm, seed_ref, step_ref,
    ig_hbm, wing_hbm, woutg_hbm,
    X, S, XT, HT, H, G, WI, WO, OG,
    PF, PB, RU, RD, C1, C2, FB, FA, SL,
    Q32, R32, CS, CR, QS, RLU, RLD, RB, FS, FR, IG,
    WS, WRU, WRD, WR, OUT,
    sems, lsem, osem,
):
    z = lax.axis_index("row")
    col = lax.axis_index("col")
    d = lax.axis_index("depth")
    core = lax.rem(col, 2)
    x = d * 2 + lax.rem(lax.div(col, 2), 2)
    y = lax.div(col, 4)

    def dev(xx, yy, zz, cc):
        xx, yy, zz = lax.rem(xx, 4), lax.rem(yy, 4), lax.rem(zz, 4)
        return {"row": zz, "col": yy * 4 + lax.rem(xx, 2) * 2 + cc, "depth": lax.div(xx, 2)}

    def first(k):
        return dev(x + k * (1 - core), y + k * core, z, core)

    def second(k):
        return dev(x + k * core, y + k * (1 - core), z, core)

    zup, zdn = dev(x, y, z + 1, core), dev(x, y, z + 3, core)
    xup, xdn = dev(x + 1, y, z, core), dev(x + 3, y, z, core)
    mate = dev(x, y, z, 1 - core)

    started = []

    def send(src, dst, to):
        k = 2 * len(started)
        copy = pltpu.make_async_remote_copy(
            src_ref=src, dst_ref=dst, send_sem=sems.at[k], recv_sem=sems.at[k + 1],
            device_id=to, device_id_type=MESH,
        )
        copy.start()
        started.append(copy)
        return copy

    def load(src, dst, k):
        c = pltpu.make_async_copy(src, dst, lsem.at[k])
        c.start()
        return c

    own = slot(0, 0, 0)
    half = pl.ds(pl.multiple_of(d * HID, HID), HID)
    other = pl.ds(pl.multiple_of((1 - d) * HID, HID), HID)
    ld_x = load(x_hbm, X.at[own, :], 0)
    ld_g = load(og_hbm, OG, 1)
    ld_wi = load(win_hbm.at[:, half], WI, 2)
    ld_wo = load(wout_hbm.at[half, :], WO, 3)

    barrier = pltpu.get_barrier_semaphore()
    near = [first(1), first(3), first(2), second(1), second(3), zup, zdn, mate]
    for n in near:
        pl.semaphore_signal(barrier, inc=1, device_id=n, device_id_type=MESH)
    pl.semaphore_wait(barrier, len(near))

    LH, RH = pl.ds(0, 768), pl.ds(768, 768)

    class Gather:
        def __init__(self, buf):
            self.buf = buf
            self.c = {}

        def spread(self, a):
            sl = self.buf.at[slot(0, 0, a), :]
            self.c[a, 1] = send(sl, self.buf.at[slot(1, 0, a), :], second(1))
            self.c[a, 3] = send(sl, self.buf.at[slot(3, 0, a), :], second(3))
            self.share(a, 0)

        def share(self, a, b):
            self.c["m", a, b] = send(self.buf.at[slot(b, 0, a), :], self.buf.at[slot(b, 1, a), :], mate)

        def begin(self):
            sl = self.buf.at[own, :]
            self.f1 = send(sl, self.buf.at[slot(0, 0, 1), :], first(1))
            self.f3 = send(sl, self.buf.at[slot(0, 0, 3), :], first(3))
            self.spread(0)

        def firsts(self):
            self.f1.wait_recv()
            l = send(self.buf.at[slot(0, 0, 1), LH], self.buf.at[slot(0, 0, 2), LH], first(1))
            self.spread(1)
            self.f3.wait_recv()
            r = send(self.buf.at[slot(0, 0, 3), RH], self.buf.at[slot(0, 0, 2), RH], first(3))
            self.spread(3)
            l.wait_recv()
            r.wait_recv()
            self.spread(2)

        def seconds(self, a):
            self.c[a, 1].wait_recv()
            self.c[a, "l"] = send(self.buf.at[slot(1, 0, a), LH], self.buf.at[slot(2, 0, a), LH], second(1))
            self.share(a, 1)
            self.c[a, 3].wait_recv()
            self.c[a, "r"] = send(self.buf.at[slot(3, 0, a), RH], self.buf.at[slot(2, 0, a), RH], second(3))
            self.share(a, 3)

        def thirds(self):
            for a in (0, 1, 3, 2):
                self.c[a, "l"].wait_recv()
                self.c[a, "r"].wait_recv()
                self.share(a, 2)

        def ready(self, b):
            for a in (0, 1, 3, 2):
                shared = self.c.pop(("m", a, b), None)
                if shared is not None:
                    shared.wait_recv()

    gx, gs = Gather(X), Gather(S)

    def mul(n):
        return pl.multiple_of(n * 256, 256)

    st = {}
    AL, AR = pl.ds(0, 384), pl.ds(384, 384)

    def quarter(k):
        return pl.ds(pl.multiple_of(lax.rem(z + k, 4) * QT, QT), QT)

    def s0(i):
        q, b = ITEMS[i]
        pf, pb = PF.at[i % 2], PB.at[i]
        rows = pl.ds(b * CH, CH)
        (gs if q else gx).ready(b)

        @pl.loop(0, 3)
        def _(n):
            cols = pl.ds(mul(n), 256)
            if q:
                r = lax.dot_general(S[rows, :], WO[cols, :], NT, preferred_element_type=F32)
            else:
                r = lax.dot_general(X[rows, :], WI[:, cols], NN, preferred_element_type=F32)
            pf[:, cols] = r
            pb[:, cols] = r.astype(BF16)

        st[i, "a1"] = send(pb.at[quarter(2), AL], RU.at[i], zup)
        st[i, "a2"] = send(pb.at[quarter(2), AR], RD.at[i], zdn)
        st[i, "b1"] = send(pb.at[quarter(1), AR], FB.at[i, :, AR], zup)
        st[i, "b2"] = send(pb.at[quarter(3), AL], FA.at[i, :, AL], zdn)

    def s1(i):
        pf = PF.at[i % 2]

        def add(relay, out, k, cols):
            base = lax.rem(z + k, 4) * QT

            @pl.loop(0, QT // 32)
            def _(j):
                o = pl.multiple_of(j * 32, 32)
                src = pl.ds(pl.multiple_of(base + o, 32), 32)
                out[pl.ds(o, 32), :] = (relay[pl.ds(o, 32), :].astype(F32) + pf[src, cols]).astype(BF16)

        st[i, "a1"].wait_recv()
        add(RU.at[i], C1.at[i], 1, AL)
        st[i, "c1"] = send(C1.at[i], FB.at[i, :, AL], zup)
        st[i, "a2"].wait_recv()
        add(RD.at[i], C2.at[i], 3, AR)
        st[i, "c2"] = send(C2.at[i], FA.at[i, :, AR], zdn)

    def s2(i):
        q, b = ITEMS[i]
        pf = PF.at[i % 2]
        for k in ("b1", "b2", "c1", "c2"):
            st[i, k].wait_recv()
        dst = G if q else H
        row0 = b * CH + z * QT

        @pl.loop(0, QT // 16)
        def _(j):
            o = pl.multiple_of(j * 16, 16)
            rr = pl.ds(o, 16)
            src = pl.ds(pl.multiple_of(z * QT + o, 16), 16)
            to = pl.ds(pl.multiple_of(row0 + o, 16), 16)
            v = pf[src, :] + FB[i, rr, :].astype(F32) + FA[i, rr, :].astype(F32)
            if q:
                dst[to, :] = (v * SL[b, rr, :]).astype(BF16)
            else:
                act, slope = gelu_parts(v)
                dst[to, :] = act.astype(BF16)
                SL[b, rr, :] = slope

        mine = dst.at[pl.ds(pl.multiple_of(row0, 16), QT), :]
        st[i, "n1"] = send(mine, mine, zup)
        st[i, "n2"] = send(mine, mine, zdn)

    def s3(i):
        q, b = ITEMS[i]
        dst = G if q else H
        up = pl.ds(pl.multiple_of(b * CH + lax.rem(z + 3, 4) * QT, 16), QT)
        dn = pl.ds(pl.multiple_of(b * CH + lax.rem(z + 1, 4) * QT, 16), QT)
        st[i, "n1"].wait_recv()
        st[i, "w1"] = send(dst.at[up, AL], dst.at[up, AL], zup)
        st[i, "n2"].wait_recv()
        st[i, "w2"] = send(dst.at[dn, AR], dst.at[dn, AR], zdn)

    def flip(src, dst, b, width):
        @pl.loop(0, width // 128)
        def _(n):
            c = pl.ds(pl.multiple_of(n * 128, 128), 128)
            dst[c, pl.ds(b * CH, CH)] = src[pl.ds(b * CH, CH), c].T

    def s4(i):
        q, b = ITEMS[i]
        st[i, "w1"].wait_recv()
        st[i, "w2"].wait_recv()
        if not q:
            flip(H, HT, b, HID)
            return
        cs = CS.at[b]

        @pl.loop(0, 6)
        def _(n):
            cols = pl.ds(mul(n), 256)
            r = lax.dot_general(G[pl.ds(b * CH, CH), :], WI[cols, :], NT, preferred_element_type=F32)
            Q32[:, cols] = r[0:192]
            cs[:, cols] = r[192:384].astype(BF16)

        st[i, "m"] = send(cs, CR.at[b], mate)

    def s5(i):
        _, b = ITEMS[i]
        st[i, "m"].wait_recv()

        @pl.loop(0, 12)
        def _(j):
            rr = pl.ds(pl.multiple_of(j * 16, 16), 16)
            v = Q32[rr, :] + CR[b, rr, :].astype(F32)
            if b:
                QS[b - 1, rr, :] = v.astype(BF16)
            else:
                R32[rr, :] = v

        if b == 1:
            st["r1"] = send(QS.at[0], RB.at[0], second(3))
        elif b == 3:
            st["r3"] = send(QS.at[2], RB.at[2], second(1))
        elif b == 2:
            st["rl"] = send(QS.at[1, :, LH], RLU, second(1))
            st["rr"] = send(QS.at[1, :, RH], RLD, second(3))

    def relay_two():
        st["rl"].wait_recv()
        st["r2l"] = send(RLU, RB.at[1, :, LH], second(1))
        st["rr"].wait_recv()
        st["r2r"] = send(RLD, RB.at[1, :, RH], second(3))

    outs = {}

    def put(k, dst):
        c = pltpu.make_async_copy(OUT.at[k % 2], dst, osem.at[k])
        c.start()
        outs[k] = c

    def w_out_away():
        @pl.loop(0, 6)
        def _(t):
            m, n = lax.div(t, 3), lax.rem(t, 3)
            rows = pl.ds(pl.multiple_of(m * 384, 384), 384)
            cols = pl.ds(pl.multiple_of((1 - d) * HID + n * 256, 256), 256)
            r = lax.dot_general(HT[rows, :], S[:, cols], NN, preferred_element_type=F32)
            WS[rows, pl.ds(mul(n), 256)] = r.astype(BF16)

        st["s1"] = send(WS.at[pl.ds(0, 384), :], WRU, xup)
        st["s2"] = send(WS.at[pl.ds(384, 384), :], WRD, xdn)

    def w_out_home(m):
        @pl.loop(0, 3)
        def _(n):
            cols = pl.ds(pl.multiple_of(d * HID + n * 256, 256), 256)
            r = lax.dot_general(HT[pl.ds(m * 384, 384), :], S[:, cols], NN, preferred_element_type=F32)
            OUT[m, :, pl.ds(mul(n), 256)] = r

        put(m, woutg_hbm.at[pl.ds(pl.multiple_of(d * HID + m * 384, 384), 384), :])

    def relay_swap():
        st["s1"].wait_recv()
        st["t1"] = send(WRU, WR.at[pl.ds(0, 384), :], xup)
        st["s2"].wait_recv()
        st["t2"] = send(WRD, WR.at[pl.ds(384, 384), :], xdn)

    def w_out_far(m):
        st["t%d" % (m + 1)].wait_recv()
        outs[m].wait()

        @pl.loop(0, 12)
        def _(j):
            o = pl.multiple_of(j * 32, 32)
            OUT[m, pl.ds(o, 32), :] = WR[pl.ds(pl.multiple_of(m * 384 + o, 32), 32), :].astype(F32)

        put(2 + m, woutg_hbm.at[pl.ds(pl.multiple_of((1 - d) * HID + m * 384, 384), 384), :])

    def w_in_part(m):
        outs[2 + m].wait()

        @pl.loop(0, 3)
        def _(n):
            cols = pl.ds(mul(n), 256)
            OUT[m % 2, :, cols] = lax.dot_general(
                XT[pl.ds(m * 384, 384), :], G[:, cols], NN, preferred_element_type=F32
            )

        put(4 + m, wing_hbm.at[pl.ds(m * 384, 384), :])

    ld_x.wait()
    gx.begin()
    ld_g.wait()
    key = mix_bits(mix_bits(step_ref[0] + jnp.int32(1013904223)) ^ seed_ref[0])
    row0 = (d * 16 + col) * OWN

    @pl.loop(0, OWN // 16)
    def _(j):
        rr = pl.ds(pl.multiple_of(j * 16, 16), 16)
        rows = lax.broadcasted_iota(I32, (16, FEAT), 0) + (row0 + j * 16)
        cols = lax.broadcasted_iota(I32, (16, FEAT), 1) + z * FEAT
        hashed = mix_bits((rows * jnp.int32(D) + cols) ^ key)
        keep = (hashed & jnp.int32(16777215)) < jnp.int32(15099494)
        v = jnp.where(keep, OG[rr, :].astype(F32) * keep_scale, jnp.zeros((), F32))
        S[rr, :] = v.astype(BF16)

    gx.firsts()
    ld_wi.wait()
    s0(0)
    gx.seconds(0)
    gx.seconds(1)
    s1(0)
    gx.seconds(3)
    gx.seconds(2)
    s0(1)
    s2(0)
    gs.begin()
    s1(1)
    gx.thirds()
    gs.firsts()
    s3(0)
    s0(2)
    s2(1)
    s1(2)
    s4(0)
    gs.seconds(0)
    gs.seconds(1)
    s3(1)
    s0(3)
    s2(2)
    s1(3)
    s4(1)
    gs.seconds(3)
    gs.seconds(2)
    s3(2)
    gs.thirds()
    ld_wo.wait()
    s0(4)
    s2(3)
    s1(4)
    s4(2)
    flip(X, XT, 0, FEAT)
    s3(3)
    s0(5)
    s2(4)
    s1(5)
    s4(3)
    gs.ready(0)
    gs.ready(3)
    w_out_away()
    s3(4)
    s0(6)
    s2(5)
    s1(6)
    s4(4)
    w_out_home(0)
    w_out_home(1)
    s3(5)
    s0(7)
    s2(6)
    s1(7)
    s5(4)
    s4(5)
    relay_swap()
    flip(X, XT, 1, FEAT)
    s3(6)
    s2(7)
    s5(5)
    s4(6)
    relay_two()
    s5(6)
    flip(X, XT, 3, FEAT)
    flip(X, XT, 2, FEAT)
    s3(7)
    s4(7)
    w_out_far(0)
    w_out_far(1)
    w_in_part(0)
    s5(7)
    for k in ("r1", "r2l", "r2r", "r3"):
        st[k].wait_recv()

    @pl.loop(0, 12)
    def _(j):
        rr = pl.ds(pl.multiple_of(j * 16, 16), 16)
        v = R32[rr, :] + RB[0, rr, :].astype(F32) + RB[1, rr, :].astype(F32) + RB[2, rr, :].astype(F32)
        R32[rr, :] = v
        FS[rr, :] = v.astype(BF16)

    st["f1"] = send(FS.at[pl.ds(OWN, OWN), :], FR.at[0], first(3))
    st["f2"] = send(FS.at[pl.ds(2 * OWN, OWN), :], FR.at[1], first(2))
    st["f3"] = send(FS.at[pl.ds(3 * OWN, OWN), :], FR.at[2], first(1))
    w_in_part(1)
    w_in_part(2)
    w_in_part(3)
    for k in ("f1", "f2", "f3"):
        st[k].wait_recv()

    @pl.loop(0, OWN // 16)
    def _(j):
        rr = pl.ds(pl.multiple_of(j * 16, 16), 16)
        IG[rr, :] = (
            R32[rr, :] + FR[0, rr, :].astype(F32) + FR[1, rr, :].astype(F32) + FR[2, rr, :].astype(F32)
        )

    fin = pltpu.make_async_copy(IG, ig_hbm, osem.at[8])
    fin.start()
    fin.wait()
    outs[6].wait()
    outs[7].wait()
    for copy in started:
        copy.wait_send()


def per_device(layer_input, w_in, w_out, out_grad, drop_seed, drop_step):
    hbm = pl.BlockSpec(memory_space=pl.ANY)
    smem = pl.BlockSpec(memory_space=pltpu.SMEM)

    def b(*shape):
        return pltpu.VMEM(shape, BF16)

    def f(*shape):
        return pltpu.VMEM(shape, F32)

    return pl.pallas_call(
        kernel,
        out_shape=(
            jax.ShapeDtypeStruct((OWN, FEAT), F32),
            jax.ShapeDtypeStruct((FEAT, HID), F32),
            jax.ShapeDtypeStruct((2 * HID, HID), F32),
        ),
        in_specs=[hbm, hbm, hbm, hbm, smem, smem],
        out_specs=(hbm, hbm, hbm),
        scratch_shapes=[
            b(1536, FEAT), b(1536, FEAT), b(FEAT, 1536), b(HID, 1536), b(1536, HID), b(1536, HID),
            b(FEAT, HID), b(HID, FEAT), b(OWN, FEAT),
            f(2, CH, HID), b(8, CH, HID), b(8, QT, 384), b(8, QT, 384), b(8, QT, 384), b(8, QT, 384),
            b(8, QT, HID), b(8, QT, HID), f(4, QT, HID),
            f(192, FEAT), f(192, FEAT), b(4, 192, FEAT), b(4, 192, FEAT), b(3, 192, FEAT),
            b(192, 768), b(192, 768), b(3, 192, FEAT), b(192, FEAT), b(3, OWN, FEAT), f(OWN, FEAT),
            b(HID, HID), b(384, HID), b(384, HID), b(HID, HID), f(2, 384, HID),
            pltpu.SemaphoreType.DMA((N_SEMS,)),
            pltpu.SemaphoreType.DMA((4,)),
            pltpu.SemaphoreType.DMA((9,)),
        ],
        compiler_params=pltpu.CompilerParams(
            collective_id=0, has_side_effects=True, vmem_limit_bytes=67_000_000
        ),
        name="mlp_backward",
    )(layer_input, w_in, w_out, out_grad, drop_seed, drop_step)


def solution(mesh):
    placed = (
        P(("depth", "col"), "row"),
        P("row", "col"),
        P("col", "row"),
        P(("depth", "col"), "row"),
        P(),
        P(),
    )
    return jax.shard_map(
        per_device,
        mesh=mesh,
        in_specs=placed,
        out_specs=(
            P(("depth", "col"), "row"),
            P("row", ("col", "depth")),
            P("col", ("row", "depth")),
        ),
        check_vma=False,
    )
```

time: 596 us -> 150 us (0.25)
  waiting for transfers between devices: 520 us -> 0 us
  Pallas kernels: 0 us -> 139 us
  matrix products: 46.2 us -> 0 us
  between operations: 15.4 us -> 1.94 us
    reduce_scatter x3 -> x0, waiting for transfers between devices: 277 us -> none  [the longest x1 119 us: per_device(): lax.psum_scatter(out_term, 'depth', scatter_dimension=1, tiled=True)]
    psum x1 -> x0, waiting for transfers between devices: 177 us -> none  [per_device(): hidden_pre, act_grad = lax.psum((partial_pre, partial_act), 'row')]
    pallas_call x0 -> x1, Pallas kernels: none -> 139 us  [per_device(): pl.pallas_call(kernel, out_shape=(jax.ShapeDtypeStruct((OWN, FEAT), F32),...]
    all_gather x2 -> x0, waiting for transfers between devices: 64.3 us -> none  [the longest x1 37.4 us: per_device(): lax.all_gather(layer_input, 'col', axis=0, tiled=True)]
    dot_general x5 -> x0, matrix products: 46.2 us -> none  [the longest x2 19.1 us: contract_rows(): lax.dot_general(left, right, (((0,), (0,)), ((), ())), preferred_element_...]
  transfers between devices with their start and end apart: 6 -> 0, of which waited for: 6 -> 0; matrix products, arithmetic and copies ran while one was open for 6% -> 0% of each run, Pallas kernels for 0% -> 0%
where the time goes in v1:
time: 150 us
  Pallas kernels  139 us (93%)
  local copies, waits for them, and re-layouts  8.92 us (6%)
  between operations  1.94 us (1%)
    pallas_call x1, Pallas kernels, per_device(): pl.pallas_call(kernel, out_shape=(jax.ShapeDtypeStruct((OWN, FEAT), F32),...  139 us
    unnamed x7, local copies, waits for them, and re-layouts  8.92 us

profile of v1, /device:TPU:1, one launch (start us, length us, event | category | flops | bytes accessed | tf_op | source)
XLA Modules:
  0.0 150.2 jit_solution(13455367351755578513)
XLA Ops:
  1.9 139.3 %mlp_backward.1 = (f32[48,1536]{1,0:T(8,128)}, f32[1536,768]{1,0:T(8,128)}, f32[1536,768]{1,0:T(8,128)}) custom-call(bf16[48,1536]{1,0:T(8,128)(2,1)} %x_hbm.1, bf16[1536,1536]{1,0:T(8,128)(2,1)} %win_hbm.1, bf16[1536,1536]{1,0:T(8,128)(2,1)} %wout_hbm.1, bf16[48,1536]{1,0:T(8,128)(2,1)} %og_hbm.1, s32[1]{0:T(128)S(6)} %copy.12.seed_ref, s32[1]{0:T(128)S(6)} %copy.13.step_ref), custom_call_target="tpu_custom_call" | custom-call | tf_op jit(solution)/shard_map/mlp_backward/pallas_call | solution.py:492
  141.3 0.0 slice-start
  141.3 1.8 %copy.14 = f32[48,1536]{1,0:T(8,128)} copy(f32[48,1536]{1,0:T(8,128)} %get-tuple-element.6) | data formatting | bytes 589824
  143.1 0.0 slice-start.1
  143.1 4.9 %copy.15 = f32[1536,768]{1,0:T(8,128)} copy(f32[1536,768]{1,0:T(8,128)} %get-tuple-element.7) | data formatting | bytes 9437184
  148.0 0.0 slice-done
  148.0 0.0 slice-done.1
  148.0 2.2 %copy.16 = f32[1536,768]{1,0:T(8,128)} copy(f32[1536,768]{1,0:T(8,128)S(1)} %bitcast.1) | data formatting | bytes 9437184
  (1 shorter events, 0.0 us)
Async XLA Ops:
  141.3 6.7 %slice-start = ((s8[4718592]{0:T(1024)(128)(4,1)}), s8[4194304]{0:T(1024)(128)(4,1)S(1)}, s32[]{:S(2)}) async-start(s8[4718592]{0:T(1024)(128)(4,1)} %bitcast), calls=%async_computation | async-start | bytes 8388608
  143.1 4.9 %slice-start.1 = ((s8[4718592]{0:T(1024)(128)(4,1)}), s8[524288]{0:T(1024)(128)(4,1)S(1)}, s32[]{:S(2)}) async-start(s8[4718592]{0:T(1024)(128)(4,1)} %bitcast), calls=%async_computation.1 | async-start | bytes 1048576

commit v2 on v1

v2 whole, which is shorter than its diff:
```python
import math

import jax
import jax.numpy as jnp
from jax import lax
from jax.experimental import pallas as pl
from jax.experimental.pallas import tpu as pltpu
from jax.sharding import PartitionSpec as P

D = 6144
keep_scale = 1.0 / 0.9
gelu_coef = math.sqrt(2.0 / math.pi)
F32, BF16, I32 = jnp.float32, jnp.bfloat16, jnp.int32
MESH = pl.DeviceIdType.MESH

OWN = 48
CH = 384
QT = 96
HID = 768
FEAT = 1536
ITEMS = [
    (0, 0, 0, 0), (0, 0, 1, 0), (0, 1, None, 1), (0, 3, None, 2), (0, 2, None, 3),
    (1, 1, None, 4), (1, 2, None, 5), (1, 3, None, 6), (1, 0, 1, 7), (1, 0, 0, 7),
]
POS = (0, 2, 1, 3)
N_SEMS = 400

NN = (((1,), (0,)), ((), ()))
NT = (((1,), (1,)), ((), ()))


def mix_bits(v):
    v = v ^ lax.shift_right_logical(v, jnp.int32(16))
    v = v * jnp.int32(2146121005)
    v = v ^ lax.shift_right_logical(v, jnp.int32(15))
    v = v * jnp.int32(-2073254261)
    v = v ^ lax.shift_right_logical(v, jnp.int32(16))
    return v


def gelu_parts(h):
    inner_arg = gelu_coef * (h + 0.044715 * h * h * h)
    t = jnp.tanh(inner_arg)
    act = 0.5 * h * (1.0 + t)
    slope = 0.5 * (1.0 + t) + 0.5 * h * (1.0 - t * t) * gelu_coef * (1.0 + 3.0 * 0.044715 * h * h)
    return act, slope


def slot(b, region, a):
    return pl.ds(((b * 2 + region) * 4 + POS[a]) * OWN, OWN)


def kernel(
    x_hbm, win_hbm, wout_hbm, og_hbm, seed_ref, step_ref,
    ig_hbm, wing_hbm, woutg_hbm,
    X, S, XT, HT, H, G, WI, WO, OG,
    PF, PB, RU, RD, C1, C2, FB, FA, SL,
    Q32, QO, CS, CR, QS, RA, QB, RB, IG,
    WS, WRU, WRD, WR, OUT, WG,
    sems, lsem, osem,
):
    z = lax.axis_index("row")
    col = lax.axis_index("col")
    d = lax.axis_index("depth")
    core = lax.rem(col, 2)
    x = d * 2 + lax.rem(lax.div(col, 2), 2)
    y = lax.div(col, 4)

    def dev(xx, yy, zz, cc):
        xx, yy, zz = lax.rem(xx, 4), lax.rem(yy, 4), lax.rem(zz, 4)
        return {"row": zz, "col": yy * 4 + lax.rem(xx, 2) * 2 + cc, "depth": lax.div(xx, 2)}

    def first(k):
        return dev(x + k * (1 - core), y + k * core, z, core)

    def second(k):
        return dev(x + k * core, y + k * (1 - core), z, core)

    zup, zdn = dev(x, y, z + 1, core), dev(x, y, z + 3, core)
    xup, xdn = dev(x + 1, y, z, core), dev(x + 3, y, z, core)
    mate = dev(x, y, z, 1 - core)

    started = []

    def send(src, dst, to):
        k = 2 * len(started)
        copy = pltpu.make_async_remote_copy(
            src_ref=src, dst_ref=dst, send_sem=sems.at[k], recv_sem=sems.at[k + 1],
            device_id=to, device_id_type=MESH,
        )
        copy.start()
        started.append(copy)
        return copy

    def load(src, dst, k):
        c = pltpu.make_async_copy(src, dst, lsem.at[k])
        c.start()
        return c

    own = slot(0, 0, 0)
    half = pl.ds(pl.multiple_of(d * HID, HID), HID)
    other = pl.ds(pl.multiple_of((1 - d) * HID, HID), HID)
    ld_x = load(x_hbm, X.at[own, :], 0)
    ld_g = load(og_hbm, OG, 1)
    ld_wi = load(win_hbm.at[:, half], WI, 2)
    ld_wo = load(wout_hbm.at[half, :], WO, 3)

    barrier = pltpu.get_barrier_semaphore()
    near = [first(1), first(3), first(2), second(1), second(3), second(2), zup, zdn, mate]
    for n in near:
        pl.semaphore_signal(barrier, inc=1, device_id=n, device_id_type=MESH)
    pl.semaphore_wait(barrier, len(near))

    LH, RH = pl.ds(0, 768), pl.ds(768, 768)

    class Gather:
        def __init__(self, buf):
            self.buf = buf
            self.c = {}

        def spread(self, a):
            sl = self.buf.at[slot(0, 0, a), :]
            self.c[a, 1] = send(sl, self.buf.at[slot(1, 0, a), :], second(1))
            self.c[a, 3] = send(sl, self.buf.at[slot(3, 0, a), :], second(3))

        def share(self, a, b):
            self.c["m", a, b] = send(self.buf.at[slot(b, 0, a), :], self.buf.at[slot(b, 1, a), :], mate)

        def begin(self):
            sl = self.buf.at[own, :]
            self.f1 = send(sl, self.buf.at[slot(0, 0, 1), :], first(1))
            self.f3 = send(sl, self.buf.at[slot(0, 0, 3), :], first(3))
            self.share(0, 0)

        def firsts(self):
            self.f1.wait_recv()
            l = send(self.buf.at[slot(0, 0, 1), LH], self.buf.at[slot(0, 0, 2), LH], first(1))
            self.share(1, 0)
            self.f3.wait_recv()
            r = send(self.buf.at[slot(0, 0, 3), RH], self.buf.at[slot(0, 0, 2), RH], first(3))
            self.share(3, 0)
            for a in (0, 1, 3):
                self.spread(a)
            self.l, self.r = l, r

        def firsts_two(self):
            self.l.wait_recv()
            self.r.wait_recv()
            self.share(2, 0)
            self.spread(2)

        def seconds(self, a):
            self.c[a, 1].wait_recv()
            self.c[a, "l"] = send(self.buf.at[slot(1, 0, a), LH], self.buf.at[slot(2, 0, a), LH], second(1))
            self.share(a, 1)
            self.c[a, 3].wait_recv()
            self.c[a, "r"] = send(self.buf.at[slot(3, 0, a), RH], self.buf.at[slot(2, 0, a), RH], second(3))
            self.share(a, 3)

        def thirds(self):
            for a in (0, 1, 3, 2):
                self.c[a, "l"].wait_recv()
                self.c[a, "r"].wait_recv()
                self.share(a, 2)

        def ready(self, b, slots=(0, 1, 3, 2)):
            for a in slots:
                shared = self.c.pop(("m", a, b), None)
                if shared is not None:
                    shared.wait_recv()

    gx, gs = Gather(X), Gather(S)

    def mul(n):
        return pl.multiple_of(n * 256, 256)

    st = {}
    AL, AR = pl.ds(0, 384), pl.ds(384, 384)

    def shape(i):
        _, b, part, k = ITEMS[i]
        rows = QT if part is None else OWN
        return b, k, rows, (part or 0) * OWN

    def quarter(k, rows):
        return pl.multiple_of(lax.rem(z + k, 4) * rows, 16)

    def tokens(buf, i, cols=None):
        b, _, rows, off = shape(i)
        if rows == QT:
            return buf[pl.ds(b * CH, CH), :]
        return jnp.concatenate([buf[pl.ds(b * CH + g * QT + off, OWN), :] for g in range(4)], axis=0)

    def s0(i):
        q = ITEMS[i][0]
        b, k, rows, off = shape(i)
        base = off * 4
        pf, pb = PF.at[i % 2], PB.at[k]
        (gs if q else gx).ready(b, (0, 1, 3, 2) if rows == QT else ((2, 3) if off else (0, 1)))

        @pl.loop(0, 3)
        def _(n):
            cols = pl.ds(mul(n), 256)
            if q:
                r = lax.dot_general(tokens(S, i), WO[cols, :], NT, preferred_element_type=F32)
            else:
                r = lax.dot_general(tokens(X, i), WI[:, cols], NN, preferred_element_type=F32)
            pf[pl.ds(0, 4 * rows), cols] = r
            pb[pl.ds(base, 4 * rows), cols] = r.astype(BF16)

        def part(j):
            return pl.ds(base + quarter(j, rows), rows)

        mine = pl.ds(off, rows)
        st[i, "a1"] = send(pb.at[part(2), AL], RU.at[k, mine], zup)
        st[i, "a2"] = send(pb.at[part(2), AR], RD.at[k, mine], zdn)
        st[i, "b1"] = send(pb.at[part(1), AR], FB.at[k, mine, AR], zup)
        st[i, "b2"] = send(pb.at[part(3), AL], FA.at[k, mine, AL], zdn)

    def s1(i):
        _, k, rows, off = shape(i)
        pf = PF.at[i % 2]
        mine = pl.ds(off, rows)

        def add(relay, out, j, cols):
            base = quarter(j, rows)

            @pl.loop(0, rows // 16)
            def _(t):
                o = pl.multiple_of(t * 16, 16)
                rr = pl.ds(off + o, 16)
                src = pl.ds(pl.multiple_of(base + o, 16), 16)
                out[rr, :] = (relay[rr, :].astype(F32) + pf[src, cols]).astype(BF16)

        st[i, "a1"].wait_recv()
        add(RU.at[k], C1.at[k], 1, AL)
        st[i, "c1"] = send(C1.at[k, mine], FB.at[k, mine, AL], zup)
        st[i, "a2"].wait_recv()
        add(RD.at[k], C2.at[k], 3, AR)
        st[i, "c2"] = send(C2.at[k, mine], FA.at[k, mine, AR], zdn)

    def s2(i):
        q = ITEMS[i][0]
        b, k, rows, off = shape(i)
        pf = PF.at[i % 2]
        for key in ("b1", "b2", "c1", "c2"):
            st[i, key].wait_recv()
        dst = G if q else H
        row0 = b * CH + z * QT + off
        base = quarter(0, rows)

        @pl.loop(0, rows // 16)
        def _(t):
            o = pl.multiple_of(t * 16, 16)
            rr = pl.ds(off + o, 16)
            src = pl.ds(pl.multiple_of(base + o, 16), 16)
            to = pl.ds(pl.multiple_of(row0 + o, 16), 16)
            v = pf[src, :] + FB[k, rr, :].astype(F32) + FA[k, rr, :].astype(F32)
            if q:
                dst[to, :] = (v * SL[b, rr, :]).astype(BF16)
            else:
                act, slope = gelu_parts(v)
                dst[to, :] = act.astype(BF16)
                SL[b, rr, :] = slope

        mine = dst.at[pl.ds(pl.multiple_of(row0, 16), rows), :]
        st[i, "n1"] = send(mine, mine, zup)
        st[i, "n2"] = send(mine, mine, zdn)

    def s3(i):
        b, _, rows, off = shape(i)
        dst = G if ITEMS[i][0] else H
        up = pl.ds(pl.multiple_of(b * CH + lax.rem(z + 3, 4) * QT + off, 16), rows)
        dn = pl.ds(pl.multiple_of(b * CH + lax.rem(z + 1, 4) * QT + off, 16), rows)
        st[i, "n1"].wait_recv()
        st[i, "w1"] = send(dst.at[up, AL], dst.at[up, AL], zup)
        st[i, "n2"].wait_recv()
        st[i, "w2"] = send(dst.at[dn, AR], dst.at[dn, AR], zdn)

    def flip(src, dst, b, width):
        @pl.loop(0, width // 128)
        def _(n):
            c = pl.ds(pl.multiple_of(n * 128, 128), 128)
            dst[c, pl.ds(b * CH, CH)] = src[pl.ds(b * CH, CH), c].T

    def s4(i):
        q, _, part, _ = ITEMS[i]
        b, _, rows, off = shape(i)
        st[i, "w1"].wait_recv()
        st[i, "w2"].wait_recv()
        if not q:
            if part != 0:
                flip(H, HT, b, HID)
            return
        cs = CS.at[b]
        mine = pl.ds(off * 2, 2 * rows)

        @pl.loop(0, 6)
        def _(n):
            cols = pl.ds(mul(n), 256)
            r = lax.dot_general(tokens(G, i), WI[cols, :], NT, preferred_element_type=F32)
            Q32[i % 2, mine, cols] = r[0 : 2 * rows]
            cs[mine, cols] = r[2 * rows : 4 * rows].astype(BF16)

        st[i, "m"] = send(cs.at[mine, :], CR.at[b, mine, :], mate)

    def s5(i):
        part = ITEMS[i][2]
        b = ITEMS[i][1]
        st[i, "m"].wait_recv()

        def add(a):
            @pl.loop(0, OWN // 16)
            def _(j):
                o = pl.multiple_of(j * 16, 16)
                rr = pl.ds(pl.multiple_of((POS[a] if part is None else a) * OWN + o, 16), 16)
                v = Q32[i % 2, rr, :] + CR[b, rr, :].astype(F32)
                if a:
                    QS[b, a - 1, pl.ds(o, 16), :] = v.astype(BF16)
                else:
                    QO[b, pl.ds(o, 16), :] = v

        for a in (2, 1, 3, 0) if part is None else ((2, 3) if part else (1, 0)):
            add(a)
            if a:
                st["q", b, a] = send(QS.at[b, a - 1], RA.at[b, a - 1], first(4 - a))

    def s6(i):
        b = ITEMS[i][1]
        for a in (1, 3, 2):
            st["q", b, a].wait_recv()
        if b == 0:
            for k in range(3):
                st["x", k].wait_recv()

        @pl.loop(0, OWN // 16)
        def _(j):
            rr = pl.ds(pl.multiple_of(j * 16, 16), 16)
            v = QO[b, rr, :] + RA[b, 0, rr, :].astype(F32) + RA[b, 1, rr, :].astype(F32) + RA[b, 2, rr, :].astype(F32)
            if b:
                QB[b - 1, rr, :] = v.astype(BF16)
            else:
                IG[rr, :] = (
                    v + RB[0, rr, :].astype(F32) + RB[1, rr, :].astype(F32) + RB[2, rr, :].astype(F32)
                )

        if b:
            st["x", b - 1] = send(QB.at[b - 1], RB.at[b - 1], second(4 - b))

    outs = {}

    def put(k, dst):
        c = pltpu.make_async_copy(OUT.at[k % 2], dst, osem.at[k])
        c.start()
        outs[k] = c

    def w_out_away():
        @pl.loop(0, 6)
        def _(t):
            m, n = lax.div(t, 3), lax.rem(t, 3)
            rows = pl.ds(pl.multiple_of(m * 384, 384), 384)
            cols = pl.ds(pl.multiple_of((1 - d) * HID + n * 256, 256), 256)
            r = lax.dot_general(HT[rows, :], S[:, cols], NN, preferred_element_type=F32)
            WS[rows, pl.ds(mul(n), 256)] = r.astype(BF16)

        for k in range(2):
            rows, down = pl.ds(k * 192, 192), pl.ds(384 + k * 192, 192)
            st["s1", k] = send(WS.at[rows, :], WRU.at[rows, :], xup)
            st["s2", k] = send(WS.at[down, :], WRD.at[rows, :], xdn)

    def w_out_home(m):
        @pl.loop(0, 3)
        def _(n):
            cols = pl.ds(pl.multiple_of(d * HID + n * 256, 256), 256)
            r = lax.dot_general(HT[pl.ds(m * 384, 384), :], S[:, cols], NN, preferred_element_type=F32)
            OUT[m, :, pl.ds(mul(n), 256)] = r

        put(m, woutg_hbm.at[pl.ds(pl.multiple_of(d * HID + m * 384, 384), 384), :])

    def relay_swap(k):
        rows, down = pl.ds(k * 192, 192), pl.ds(384 + k * 192, 192)
        st["s1", k].wait_recv()
        st["t", 0, k] = send(WRU.at[rows, :], WR.at[rows, :], xup)
        st["s2", k].wait_recv()
        st["t", 1, k] = send(WRD.at[rows, :], WR.at[down, :], xdn)

    def w_out_far(m):
        for k in range(2):
            st["t", m, k].wait_recv()
        outs[m].wait()

        @pl.loop(0, 12)
        def _(j):
            o = pl.multiple_of(j * 32, 32)
            OUT[m, pl.ds(o, 32), :] = WR[pl.ds(pl.multiple_of(m * 384 + o, 32), 32), :].astype(F32)

        put(2 + m, woutg_hbm.at[pl.ds(pl.multiple_of((1 - d) * HID + m * 384, 384), 384), :])

    def w_in_most(m):
        rows = pl.ds(m * 384, 384)

        @pl.loop(0, 3)
        def _(n):
            cols = pl.ds(mul(n), 256)
            WG[rows, cols] = lax.dot_general(
                XT[rows, pl.ds(CH, 3 * CH)], G[pl.ds(CH, 3 * CH), cols], NN, preferred_element_type=F32
            )

    def w_in_rest(m):
        rows = pl.ds(m * 384, 384)

        @pl.loop(0, 3)
        def _(n):
            cols = pl.ds(mul(n), 256)
            WG[rows, cols] += lax.dot_general(
                XT[rows, pl.ds(0, CH)], G[pl.ds(0, CH), cols], NN, preferred_element_type=F32
            )

        outs[4 + m] = pltpu.make_async_copy(WG.at[rows, :], wing_hbm.at[rows, :], osem.at[4 + m])
        outs[4 + m].start()

    ld_x.wait()
    gx.begin()
    ld_g.wait()
    key = mix_bits(mix_bits(step_ref[0] + jnp.int32(1013904223)) ^ seed_ref[0])
    row0 = (d * 16 + col) * OWN

    @pl.loop(0, OWN // 16)
    def _(j):
        rr = pl.ds(pl.multiple_of(j * 16, 16), 16)
        rows = lax.broadcasted_iota(I32, (16, FEAT), 0) + (row0 + j * 16)
        cols = lax.broadcasted_iota(I32, (16, FEAT), 1) + z * FEAT
        hashed = mix_bits((rows * jnp.int32(D) + cols) ^ key)
        keep = (hashed & jnp.int32(16777215)) < jnp.int32(15099494)
        v = jnp.where(keep, OG[rr, :].astype(F32) * keep_scale, jnp.zeros((), F32))
        S[rr, :] = v.astype(BF16)

    gx.firsts()
    ld_wi.wait()
    s0(0)
    gx.firsts_two()
    s0(1)
    s1(0)
    gx.seconds(0)
    gx.seconds(1)
    gx.seconds(3)
    s1(1)
    s2(0)
    gx.seconds(2)
    s2(1)
    s0(2)
    s3(0)
    s3(1)
    s1(2)
    gx.thirds()
    gs.begin()
    s0(3)
    s2(2)
    s4(0)
    s4(1)
    s1(3)
    gs.firsts()
    s3(2)
    gs.firsts_two()
    s0(4)
    s2(3)
    s4(2)
    s1(4)
    gs.seconds(0)
    gs.seconds(1)
    s3(3)
    gs.seconds(3)
    gs.seconds(2)
    ld_wo.wait()
    s0(5)
    s2(4)
    s4(3)
    s1(5)
    gs.thirds()
    flip(X, XT, 0, FEAT)
    s3(4)
    s0(6)
    s2(5)
    flip(X, XT, 1, FEAT)
    s4(4)
    s1(6)
    gs.ready(0)
    gs.ready(3)
    w_out_away()
    s3(5)
    s0(7)
    s2(6)
    s4(5)
    s1(7)
    w_out_home(0)
    relay_swap(0)
    s3(6)
    s0(8)
    s2(7)
    s5(5)
    flip(X, XT, 2, FEAT)
    s1(8)
    relay_swap(1)
    s0(9)
    s4(6)
    s3(7)
    s2(8)
    s1(9)
    flip(X, XT, 3, FEAT)
    s3(8)
    s5(6)
    s6(5)
    s2(9)
    s4(7)
    w_in_most(0)
    s3(9)
    s5(7)
    s4(8)
    w_in_most(1)
    s4(9)
    s6(6)
    w_in_most(2)
    s5(8)
    s5(9)
    s6(7)
    w_out_home(1)
    w_in_rest(0)
    w_in_rest(1)
    w_in_rest(2)
    w_in_most(3)
    w_in_rest(3)
    s6(9)
    w_out_far(0)
    w_out_far(1)
    fin = pltpu.make_async_copy(IG, ig_hbm, osem.at[8])
    fin.start()
    fin.wait()
    for m in range(2, 8):
        outs[m].wait()
    for copy in started:
        copy.wait_send()


def per_device(layer_input, w_in, w_out, out_grad, drop_seed, drop_step):
    hbm = pl.BlockSpec(memory_space=pl.ANY)
    smem = pl.BlockSpec(memory_space=pltpu.SMEM)

    def b(*shape):
        return pltpu.VMEM(shape, BF16)

    def f(*shape):
        return pltpu.VMEM(shape, F32)

    return pl.pallas_call(
        kernel,
        out_shape=(
            jax.ShapeDtypeStruct((OWN, FEAT), F32),
            jax.ShapeDtypeStruct((FEAT, HID), F32),
            jax.ShapeDtypeStruct((2 * HID, HID), F32),
        ),
        in_specs=[hbm, hbm, hbm, hbm, smem, smem],
        out_specs=(hbm, hbm, hbm),
        scratch_shapes=[
            b(1536, FEAT), b(1536, FEAT), b(FEAT, 1536), b(HID, 1536), b(1536, HID), b(1536, HID),
            b(FEAT, HID), b(HID, FEAT), b(OWN, FEAT),
            f(2, CH, HID), b(8, CH, HID), b(8, QT, 384), b(8, QT, 384), b(8, QT, 384), b(8, QT, 384),
            b(8, QT, HID), b(8, QT, HID), f(4, QT, HID),
            f(2, 192, FEAT), f(4, OWN, FEAT), b(4, 192, FEAT), b(4, 192, FEAT), b(4, 3, OWN, FEAT),
            b(4, 3, OWN, FEAT), b(3, OWN, FEAT), b(3, OWN, FEAT), f(OWN, FEAT),
            b(HID, HID), b(384, HID), b(384, HID), b(HID, HID), f(2, 384, HID), f(FEAT, HID),
            pltpu.SemaphoreType.DMA((N_SEMS,)),
            pltpu.SemaphoreType.DMA((4,)),
            pltpu.SemaphoreType.DMA((9,)),
        ],
        compiler_params=pltpu.CompilerParams(
            collective_id=0, has_side_effects=True, vmem_limit_bytes=67_000_000
        ),
        name="mlp_backward",
    )(layer_input, w_in, w_out, out_grad, drop_seed, drop_step)


def solution(mesh):
    placed = (
        P(("depth", "col"), "row"),
        P("row", "col"),
        P("col", "row"),
        P(("depth", "col"), "row"),
        P(),
        P(),
    )
    return jax.shard_map(
        per_device,
        mesh=mesh,
        in_specs=placed,
        out_specs=(
            P(("depth", "col"), "row"),
            P("row", ("col", "depth")),
            P("col", ("row", "depth")),
        ),
        check_vma=False,
    )
```

time: 150 us -> 136 us (0.907)
  Pallas kernels: 139 us -> 125 us
    pallas_call x1, Pallas kernels: 139 us -> 125 us  [per_device(): pl.pallas_call(kernel, out_shape=(jax.ShapeDtypeStruct((OWN, FEAT), F32),...]
where the time goes in v2:
time: 136 us
  Pallas kernels  125 us (92%)
  local copies, waits for them, and re-layouts  8.92 us (7%)
  between operations  1.94 us (1%)
    pallas_call x1, Pallas kernels, per_device(): pl.pallas_call(kernel, out_shape=(jax.ShapeDtypeStruct((OWN, FEAT), F32),...  125 us
    unnamed x7, local copies, waits for them, and re-layouts  8.92 us

profile of v2, /device:TPU:1, one launch (start us, length us, event | category | flops | bytes accessed | tf_op | source)
XLA Modules:
  0.0 136.3 jit_solution(6204665417629915358)
XLA Ops:
  1.9 125.4 %mlp_backward.1 = (f32[48,1536]{1,0:T(8,128)}, f32[1536,768]{1,0:T(8,128)}, f32[1536,768]{1,0:T(8,128)}) custom-call(bf16[48,1536]{1,0:T(8,128)(2,1)} %x_hbm.1, bf16[1536,1536]{1,0:T(8,128)(2,1)} %win_hbm.1, bf16[1536,1536]{1,0:T(8,128)(2,1)} %wout_hbm.1, bf16[48,1536]{1,0:T(8,128)(2,1)} %og_hbm.1, s32[1]{0:T(128)S(6)} %copy.12.seed_ref, s32[1]{0:T(128)S(6)} %copy.13.step_ref), custom_call_target="tpu_custom_call" | custom-call | tf_op jit(solution)/shard_map/mlp_backward/pallas_call | solution.py:554
  127.4 0.0 slice-start
  127.4 1.8 %copy.14 = f32[48,1536]{1,0:T(8,128)} copy(f32[48,1536]{1,0:T(8,128)} %get-tuple-element.6) | data formatting | bytes 589824
  129.2 0.0 slice-start.1
  129.2 4.9 %copy.15 = f32[1536,768]{1,0:T(8,128)} copy(f32[1536,768]{1,0:T(8,128)} %get-tuple-element.7) | data formatting | bytes 9437184
  134.1 0.0 slice-done
  134.1 0.0 slice-done.1
  134.1 2.2 %copy.16 = f32[1536,768]{1,0:T(8,128)} copy(f32[1536,768]{1,0:T(8,128)S(1)} %bitcast.1) | data formatting | bytes 9437184
  (1 shorter events, 0.0 us)
Async XLA Ops:
  127.4 6.7 %slice-start = ((s8[4718592]{0:T(1024)(128)(4,1)}), s8[4194304]{0:T(1024)(128)(4,1)S(1)}, s32[]{:S(2)}) async-start(s8[4718592]{0:T(1024)(128)(4,1)} %bitcast), calls=%async_computation | async-start | bytes 8388608
  129.2 4.9 %slice-start.1 = ((s8[4718592]{0:T(1024)(128)(4,1)}), s8[524288]{0:T(1024)(128)(4,1)S(1)}, s32[]{:S(2)}) async-start(s8[4718592]{0:T(1024)(128)(4,1)} %bitcast), calls=%async_computation.1 | async-start | bytes 1048576

commit v3 on v2

--- a/solution.py
+++ b/solution.py
@@ -52,12 +52,12 @@
 
 def kernel(
     x_hbm, win_hbm, wout_hbm, og_hbm, seed_ref, step_ref,
-    ig_hbm, wing_hbm, woutg_hbm,
+    IG, WG, WOG,
     X, S, XT, HT, H, G, WI, WO, OG,
     PF, PB, RU, RD, C1, C2, FB, FA, SL,
-    Q32, QO, CS, CR, QS, RA, QB, RB, IG,
-    WS, WRU, WRD, WR, OUT, WG,
-    sems, lsem, osem,
+    Q32, QO, CS, CR, QS, RA, QB, RB,
+    WS, WRU, WRD, WR,
+    sems, lsem,
 ):
     z = lax.axis_index("row")
     col = lax.axis_index("col")
@@ -347,13 +347,6 @@
         if b:
             st["x", b - 1] = send(QB.at[b - 1], RB.at[b - 1], second(4 - b))
 
-    outs = {}
-
-    def put(k, dst):
-        c = pltpu.make_async_copy(OUT.at[k % 2], dst, osem.at[k])
-        c.start()
-        outs[k] = c
-
     def w_out_away():
         @pl.loop(0, 6)
         def _(t):
@@ -373,9 +366,7 @@
         def _(n):
             cols = pl.ds(pl.multiple_of(d * HID + n * 256, 256), 256)
             r = lax.dot_general(HT[pl.ds(m * 384, 384), :], S[:, cols], NN, preferred_element_type=F32)
-            OUT[m, :, pl.ds(mul(n), 256)] = r
-
-        put(m, woutg_hbm.at[pl.ds(pl.multiple_of(d * HID + m * 384, 384), 384), :])
+            WOG[pl.ds(pl.multiple_of(d * HID + m * 384, 384), 384), pl.ds(mul(n), 256)] = r
 
     def relay_swap(k):
         rows, down = pl.ds(k * 192, 192), pl.ds(384 + k * 192, 192)
@@ -387,14 +378,12 @@
     def w_out_far(m):
         for k in range(2):
             st["t", m, k].wait_recv()
-        outs[m].wait()
 
         @pl.loop(0, 12)
         def _(j):
             o = pl.multiple_of(j * 32, 32)
-            OUT[m, pl.ds(o, 32), :] = WR[pl.ds(pl.multiple_of(m * 384 + o, 32), 32), :].astype(F32)
-
-        put(2 + m, woutg_hbm.at[pl.ds(pl.multiple_of((1 - d) * HID + m * 384, 384), 384), :])
+            to = pl.ds(pl.multiple_of((1 - d) * HID + m * 384 + o, 32), 32)
+            WOG[to, :] = WR[pl.ds(pl.multiple_of(m * 384 + o, 32), 32), :].astype(F32)
 
     def w_in_most(m):
         rows = pl.ds(m * 384, 384)
@@ -415,9 +404,6 @@
             WG[rows, cols] += lax.dot_general(
                 XT[rows, pl.ds(0, CH)], G[pl.ds(0, CH), cols], NN, preferred_element_type=F32
             )
-
-        outs[4 + m] = pltpu.make_async_copy(WG.at[rows, :], wing_hbm.at[rows, :], osem.at[4 + m])
-        outs[4 + m].start()
 
     ld_x.wait()
     gx.begin()
@@ -532,11 +518,6 @@
     s6(9)
     w_out_far(0)
     w_out_far(1)
-    fin = pltpu.make_async_copy(IG, ig_hbm, osem.at[8])
-    fin.start()
-    fin.wait()
-    for m in range(2, 8):
-        outs[m].wait()
     for copy in started:
         copy.wait_send()
 
@@ -554,26 +535,25 @@
     return pl.pallas_call(
         kernel,
         out_shape=(
-            jax.ShapeDtypeStruct((OWN, FEAT), F32),
-            jax.ShapeDtypeStruct((FEAT, HID), F32),
-            jax.ShapeDtypeStruct((2 * HID, HID), F32),
+            pltpu.VMEM((OWN, FEAT), F32),
+            pltpu.VMEM((FEAT, HID), F32),
+            pltpu.VMEM((2 * HID, HID), F32),
         ),
         in_specs=[hbm, hbm, hbm, hbm, smem, smem],
-        out_specs=(hbm, hbm, hbm),
+        out_specs=(pl.BlockSpec(memory_space=pltpu.VMEM),) * 3,
         scratch_shapes=[
             b(1536, FEAT), b(1536, FEAT), b(FEAT, 1536), b(HID, 1536), b(1536, HID), b(1536, HID),
             b(FEAT, HID), b(HID, FEAT), b(OWN, FEAT),
             f(2, CH, HID), b(8, CH, HID), b(8, QT, 384), b(8, QT, 384), b(8, QT, 384), b(8, QT, 384),
             b(8, QT, HID), b(8, QT, HID), f(4, QT, HID),
             f(2, 192, FEAT), f(4, OWN, FEAT), b(4, 192, FEAT), b(4, 192, FEAT), b(4, 3, OWN, FEAT),
-            b(4, 3, OWN, FEAT), b(3, OWN, FEAT), b(3, OWN, FEAT), f(OWN, FEAT),
-            b(HID, HID), b(384, HID), b(384, HID), b(HID, HID), f(2, 384, HID), f(FEAT, HID),
+            b(4, 3, OWN, FEAT), b(3, OWN, FEAT), b(3, OWN, FEAT),
+            b(HID, HID), b(384, HID), b(384, HID), b(HID, HID),
             pltpu.SemaphoreType.DMA((N_SEMS,)),
             pltpu.SemaphoreType.DMA((4,)),
-            pltpu.SemaphoreType.DMA((9,)),
         ],
         compiler_params=pltpu.CompilerParams(
-            collective_id=0, has_side_effects=True, vmem_limit_bytes=67_000_000
+            collective_id=0, has_side_effects=True, vmem_limit_bytes=56_500_000
         ),
         name="mlp_backward",
     )(layer_input, w_in, w_out, out_grad, drop_seed, drop_step)

time: 136 us -> 131 us (0.963)
  local copies, waits for them, and re-layouts: 8.92 us -> 5.09 us
    unnamed x7 -> x3, local copies, waits for them, and re-layouts: 8.92 us -> 5.09 us
    pallas_call x1, Pallas kernels: 125 us -> 124 us  [per_device(): pl.pallas_call(kernel, out_shape=(pltpu.VMEM((OWN, FEAT), F32), pltpu.VME...]
where the time goes in v3:
time: 131 us
  Pallas kernels  124 us (95%)
  local copies, waits for them, and re-layouts  5.09 us (4%)
  between operations  1.93 us (1%)
    pallas_call x1, Pallas kernels, per_device(): pl.pallas_call(kernel, out_shape=(pltpu.VMEM((OWN, FEAT), F32), pltpu.VME...  124 us
    unnamed x3, local copies, waits for them, and re-layouts  5.09 us

profile of v3, /device:TPU:1, one launch (start us, length us, event | category | flops | bytes accessed | tf_op | source)
XLA Modules:
  0.0 131.0 jit_solution(1514075202779493846)
XLA Ops:
  1.9 123.9 %mlp_backward.1 = (f32[48,1536]{1,0:T(8,128)S(1)}, f32[1536,768]{1,0:T(8,128)S(1)}, f32[1536,768]{1,0:T(8,128)S(1)}) custom-call(bf16[48,1536]{1,0:T(8,128)(2,1)} %x_hbm.1, bf16[1536,1536]{1,0:T(8,128)(2,1)} %win_hbm.1, bf16[1536,1536]{1,0:T(8,128)(2,1)} %wout_hbm.1, bf16[48,1536]{1,0:T(8,128)(2,1)} %og_hbm.1, s32[1]{0:T(128)S(6)} %copy.15.seed_ref, ...), custom_call_target="tpu_custom_call" | custom-call | tf_op jit(solution)/shard_map/mlp_backward/pallas_call | solution.py:535
  125.9 0.7 copy.12
  126.6 2.2 %copy.13 = f32[1536,768]{1,0:T(8,128)} copy(f32[1536,768]{1,0:T(8,128)S(1)} %get-tuple-element.4) | data formatting | bytes 9437184
  128.8 2.2 %copy.14 = f32[1536,768]{1,0:T(8,128)} copy(f32[1536,768]{1,0:T(8,128)S(1)} %get-tuple-element.5) | data formatting | bytes 9437184

commit v4 on v3

--- a/solution.py
+++ b/solution.py
@@ -493,31 +493,31 @@
     s2(8)
     s1(9)
     flip(X, XT, 3, FEAT)
+    w_out_home(1)
     s3(8)
+    s2(9)
     s5(6)
+    s4(7)
     s6(5)
-    s2(9)
-    s4(7)
     w_in_most(0)
+    s5(7)
     s3(9)
-    s5(7)
     s4(8)
     w_in_most(1)
+    s5(8)
+    s6(6)
     s4(9)
-    s6(6)
+    s6(7)
     w_in_most(2)
-    s5(8)
     s5(9)
-    s6(7)
-    w_out_home(1)
     w_in_rest(0)
     w_in_rest(1)
     w_in_rest(2)
     w_in_most(3)
     w_in_rest(3)
-    s6(9)
     w_out_far(0)
     w_out_far(1)
+    s6(9)
     for copy in started:
         copy.wait_send()
 

time: 131 us -> 129 us (0.985)
  Pallas kernels: 124 us -> 121 us
    pallas_call x1, Pallas kernels: 124 us -> 121 us  [per_device(): pl.pallas_call(kernel, out_shape=(pltpu.VMEM((OWN, FEAT), F32), pltpu.VME...]
where the time goes in v4:
time: 129 us; the launch traced here: 128 us
  Pallas kernels  121 us (94%)
  local copies, waits for them, and re-layouts  5.09 us (4%)
  between operations  1.93 us (1%)
    pallas_call x1, Pallas kernels, per_device(): pl.pallas_call(kernel, out_shape=(pltpu.VMEM((OWN, FEAT), F32), pltpu.VME...  121 us
    unnamed x3, local copies, waits for them, and re-layouts  5.09 us

profile of v4, /device:TPU:1, one launch (start us, length us, event | category | flops | bytes accessed | tf_op | source)
XLA Modules:
  0.0 128.4 jit_solution(1641294442708883830)
XLA Ops:
  1.9 121.4 %mlp_backward.1 = (f32[48,1536]{1,0:T(8,128)S(1)}, f32[1536,768]{1,0:T(8,128)S(1)}, f32[1536,768]{1,0:T(8,128)S(1)}) custom-call(bf16[48,1536]{1,0:T(8,128)(2,1)} %x_hbm.1, bf16[1536,1536]{1,0:T(8,128)(2,1)} %win_hbm.1, bf16[1536,1536]{1,0:T(8,128)(2,1)} %wout_hbm.1, bf16[48,1536]{1,0:T(8,128)(2,1)} %og_hbm.1, s32[1]{0:T(128)S(6)} %copy.15.seed_ref, ...), custom_call_target="tpu_custom_call" | custom-call | tf_op jit(solution)/shard_map/mlp_backward/pallas_call | solution.py:535
  123.3 0.7 copy.12
  124.0 2.2 %copy.13 = f32[1536,768]{1,0:T(8,128)} copy(f32[1536,768]{1,0:T(8,128)S(1)} %get-tuple-element.4) | data formatting | bytes 9437184
  126.2 2.2 %copy.14 = f32[1536,768]{1,0:T(8,128)} copy(f32[1536,768]{1,0:T(8,128)S(1)} %get-tuple-element.5) | data formatting | bytes 9437184
